TPU v7x, 32 devices: a whole 2x2x4 slice. The times are simulated.
32 devices in a mesh: req: 8 (over z, y), tp: 4 (over x, core).
Axes of the slice: x: 2, y: 2, z: 4, core: 2. Of those that a mesh axis runs over, the one named last changes fastest.
Arguments:
- tokens: bfloat16 [16, 256, 2048], P('req'), may hold values from -6 to 6
- attn_gain: float32 [2048], replicated, may hold values from 0.25 to 1.75
- w_query: bfloat16 [2048, 1280], P(None, 'tp'), may hold values from -0.125 to 0.125
- key_value_weight: bfloat16 [2048, 640], replicated, may hold values from -0.125 to 0.125
- w_out: bfloat16 [1280, 2048], P('tp'), may hold values from -0.15625 to 0.15625
- q_gain: float32 [64], replicated, as said below
- k_gain: float32 [64], replicated, as said below
- stored: bfloat16 [8, 5, 2048, 128], P('req'), may hold values from -6 to 6
- continuing: int32 [16], replicated, may hold values from 0 to 1, as said below
- cache_row: int32 [16], replicated, may hold values from -1 to 7, as said below
- cache_len: int32 [16], replicated, may hold values from 0 to 2048, as said below
Outputs:
- layer: bfloat16 [16, 256, 2048], P('req')
- decoding_group_cache: bfloat16 [32, 5, 1152, 128], P('req', None, 'tp')
Inputs may be any that keep to these rules, and one draw needn't show every extreme that they name: `continuing`: exactly 8 requests have 1. `cache_row`: a continuing request's row of stored; every row belongs to exactly one continuing request; -1 for the others. `cache_len`: 1 to 2048 for a continuing request, 2048 for at least one; 0 for the others. `q_gain`: positive. `k_gain`: positive.
All inputs are finite; a program needn't handle non-finite values.
Results may differ from a plain program's by a relative error of at most 0.005.
The roundings to bfloat16 on the way count: a program that leaves them out, or rounds other values in their place, can miss the bound.
Values may be sent and summed in bfloat16 or wider, within the bound.
No kernel may reach another device: no remote copies, remote signals or barrier semaphores. Data moves between devices by JAX's collectives and lax.ppermute only.
A program may use at most 128 MiB of HBM per device.

v0:
```python
import math
import jax
import jax.numpy as jnp
from jax import lax
from jax.sharding import PartitionSpec as P


def swapped(value, axis, apart):
    mask = 2**apart
    pairs = [(source, source ^ mask) for source in range(lax.axis_size(axis))]
    return lax.ppermute(value, axis, pairs)


def normalize(values, gain):
    return values * lax.rsqrt(jnp.mean(values * values, axis=-1, keepdims=True) + 1e-06) * gain


def rotary(values, positions):
    half_dim = values.shape[-1] // 2
    freq = jnp.exp(
        -math.log(10000.0) * jnp.arange(half_dim).astype(jnp.float32) * 2.0 / values.shape[-1]
    )
    angle = positions.astype(jnp.float32)[..., None] * freq
    cosine = jnp.cos(angle)[..., None, :]
    sine = jnp.sin(angle)[..., None, :]
    first_half = values[..., :half_dim]
    second_half = values[..., half_dim:]
    return jnp.concatenate(
        [first_half * cosine - second_half * sine, second_half * cosine + first_half * sine],
        axis=-1,
    )


def attend(query_one, keys_one, allowed, head_dim, new_count, scale):
    scores = (
        jnp.einsum(
            "hqd,hkd->hqk", query_one, keys_one[..., :head_dim], preferred_element_type=jnp.float32
        )
        * scale
    )
    scores = jnp.where(allowed[None], scores, -jnp.inf)
    row_max = jnp.max(scores, axis=-1, keepdims=True)
    weights = jnp.exp(scores - row_max)
    probs = (weights / jnp.sum(weights, axis=-1, keepdims=True)).astype(jnp.bfloat16)
    mixed = jnp.einsum(
        "hqk,hkd->qhd", probs, keys_one[..., head_dim:], preferred_element_type=jnp.float32
    )
    return mixed.astype(jnp.bfloat16).reshape(new_count, query_one.shape[0] * head_dim)


def on_device(
    tokens,
    attn_gain,
    w_query,
    key_value_weight,
    w_out,
    q_gain,
    k_gain,
    stored,
    continuing,
    cache_row,
    cache_len,
):
    tp_count = lax.axis_size("tp")
    req_place = lax.axis_index("req")
    tp_place = lax.axis_index("tp")
    req_dev, new_count, width = tokens.shape
    head_dim = q_gain.shape[0]
    kv_heads = key_value_weight.shape[1] // (2 * head_dim)
    local_heads = w_query.shape[1] // head_dim
    query_group_ratio = local_heads * tp_count // kv_heads
    cache_span = stored.shape[2]
    total_length = cache_span + new_count
    scale = 1.0 / math.sqrt(head_dim)
    relayed = lax.all_to_all(stored, "req", split_axis=2, concat_axis=0, tiled=True)
    live_all = continuing == 1
    rows_all = jnp.where(live_all, cache_row, 0)
    select_chosen = jnp.take(relayed, rows_all, axis=0)
    stored_entries = lax.all_to_all(
        jnp.where(live_all[:, None, None, None], select_chosen, jnp.zeros_like(select_chosen)),
        "req",
        split_axis=0,
        concat_axis=2,
        tiled=True,
    )
    first = req_place * req_dev
    my_live = lax.dynamic_slice_in_dim(continuing, first, req_dev) == 1
    my_len = jnp.where(my_live, lax.dynamic_slice_in_dim(cache_len, first, req_dev), 0)
    position = jnp.arange(cache_span, dtype=jnp.int32)
    stored_entries = jnp.where(
        (position[None, :] < my_len[:, None])[:, None, :, None],
        stored_entries,
        jnp.zeros_like(stored_entries),
    )
    token_rows = tokens.reshape(req_dev * new_count, width)
    normalized_input = normalize(token_rows.astype(jnp.float32), attn_gain).astype(jnp.bfloat16)
    positions = my_len[:, None] + jnp.arange(new_count, dtype=jnp.int32)[None, :]
    query = jnp.dot(normalized_input, w_query, preferred_element_type=jnp.float32).reshape(
        req_dev, new_count, local_heads, head_dim
    )
    query = rotary(normalize(query, q_gain), positions).astype(jnp.bfloat16)
    key_value_rows = jnp.dot(
        normalized_input, key_value_weight, preferred_element_type=jnp.float32
    ).reshape(req_dev, new_count, kv_heads, 2 * head_dim)
    keys_new = rotary(normalize(key_value_rows[..., :head_dim], k_gain), positions)
    fresh = jnp.concatenate([keys_new, key_value_rows[..., head_dim:]], axis=-1).astype(
        jnp.bfloat16
    )
    fresh = jnp.transpose(fresh, (0, 2, 1, 3))
    keys_all = jnp.concatenate([stored_entries, fresh], axis=2)
    head_select = (
        tp_place * local_heads + jnp.arange(local_heads, dtype=jnp.int32)
    ) // query_group_ratio
    query_index = jnp.arange(new_count, dtype=jnp.int32)[:, None]
    key_index = jnp.arange(total_length, dtype=jnp.int32)[None, :]
    outputs = []
    for number in range(req_dev):
        query_one = jnp.transpose(query[number], (1, 0, 2))
        chosen = jnp.take(keys_all[number], head_select, axis=0)
        allowed = jnp.where(
            key_index < cache_span,
            key_index < my_len[number],
            key_index - cache_span <= query_index,
        )
        mixed = attend(query_one, chosen, allowed, head_dim, new_count, scale)
        outputs.append(mixed)
    mixed_all = jnp.concatenate(outputs, axis=0)
    summed = lax.psum(jnp.dot(mixed_all, w_out, preferred_element_type=jnp.float32), "tp")
    layer = (token_rows.astype(jnp.float32) + summed).astype(jnp.bfloat16)
    layer = layer.reshape(req_dev, new_count, width)
    padded_tokens = jnp.concatenate(
        [stored_entries, jnp.zeros((req_dev, kv_heads, new_count, 2 * head_dim), jnp.bfloat16)],
        axis=2,
    )
    whole = jax.vmap(
        lambda padded_one, fresh_one, offset: lax.dynamic_update_slice_in_dim(
            padded_one, fresh_one, offset, 1
        )
    )(padded_tokens, fresh, my_len)
    half_span = total_length // 2
    segment = half_span // tp_count
    pair_side = req_place % 2
    kept_half = lax.dynamic_slice_in_dim(
        whole, pair_side * half_span + tp_place * segment, segment, 2
    )
    sent_half = lax.dynamic_slice_in_dim(
        whole, (1 - pair_side) * half_span + tp_place * segment, segment, 2
    )
    partner = swapped(sent_half, "req", 0)
    decoding_group_cache = jnp.where(
        pair_side == 0,
        jnp.concatenate([kept_half, partner], axis=0),
        jnp.concatenate([partner, kept_half], axis=0),
    )
    return (layer, decoding_group_cache)


def solution(mesh):
    return jax.shard_map(
        on_device,
        mesh=mesh,
        in_specs=(
            P("req", None, None),
            P(),
            P(None, "tp"),
            P(),
            P("tp", None),
            P(),
            P(),
            P("req", None, None, None),
            P(),
            P(),
            P(),
        ),
        out_specs=(P("req", None, None), P("req", None, "tp", None)),
        check_vma=False,
    )
```

profile of v0, /device:TPU:0, one launch (start us, length us, event | category | flops | bytes accessed | tf_op | source)
XLA Modules:
  0.0 405.0 jit_solution(1439324511392412007)
XLA Ops:
  7.2 5.2 %copy.40 = bf16[1,5,2048,128]{3,1,0,2:T(8,128)(2,1)} copy(bf16[1,5,2048,128]{3,2,1,0:T(8,128)(2,1)} %param.20) | data formatting | bytes 5242880 | tf_op args[7]
  12.4 7.4 %all-to-all-start = ((bf16[1,5,2048,128]{3,1,0,2:T(8,128)(2,1)}), bf16[1,5,2048,128]{3,1,0,2:T(8,128)(2,1)}, u32[]{:S(2)}, u32[]{:S(2)}) async-start(bf16[1,5,2048,128]{3,1,0,2:T(8,128)(2,1)} %copy.40), calls=%async_computation | async-start | bytes 8388608 | tf_op jit(solution)/shard_map/all_to_all | solution.py:75
  19.9 93.2 %all-to-all-done = bf16[1,5,2048,128]{3,1,0,2:T(8,128)(2,1)} async-done(((bf16[1,5,2048,128]{3,1,0,2:T(8,128)(2,1)}), bf16[1,5,2048,128]{3,1,0,2:T(8,128)(2,1)}, u32[]{:S(2)}, u32[]{:S(2)}) %all-to-all-start) | async-done | bytes 2621472 | tf_op jit(solution)/shard_map/all_to_all | solution.py:75
  113.1 4.4 %copy.54 = bf16[1,5,8,256,128]{4,3,1,2,0:T(8,128)(2,1)} copy(bf16[1,5,8,256,128]{4,1,3,2,0:T(8,128)(2,1)} %bitcast.1) | data formatting | bytes 5242880 | tf_op jit(solution)/shard_map/all_to_all | solution.py:75
  117.6 5.3 %gather_fusion = bf16[16,5,256,128]{3,2,1,0:T(8,128)(2,1)} fusion(bf16[8,5,256,128]{3,2,1,0:T(8,128)(2,1)} %bitcast.95, s32[1024]{0:T(1024)S(1)} %pad_clamp_fusion.1), kind=kCustom, calls=%fused_computation.2 | custom fusion | bytes 10485824 | tf_op jit(solution)/shard_map/jit(_take)/gather | solution.py:78
  122.9 5.5 %select_select_fusion = bf16[16,5,256,128]{3,2,1,0:T(8,128)(2,1)} fusion(bf16[16,5,256,128]{3,2,1,0:T(8,128)(2,1)} %gather_fusion, pred[16]{0:T(512)(128)(4,1)S(1)} %get-tuple-element.41, pred[16]{0:T(512)(128)(4,1)S(1)} %get-tuple-element.65), kind=kLoop, calls=%fused_computation.27 | loop fusion | flops 5242880 | bytes 10485792 | tf_op jit(solution)/shard_map/jit(_where)/select_n | solution.py:80
  128.3 4.6 %all-to-all-start.1 = ((bf16[16,5,256,128]{3,2,1,0:T(8,128)(2,1)}), bf16[16,5,256,128]{3,2,1,0:T(8,128)(2,1)}, u32[]{:S(2)}, u32[]{:S(2)}) async-start(bf16[16,5,256,128]{3,2,1,0:T(8,128)(2,1)} %select_select_fusion), calls=%async_computation.1 | async-start | bytes 10485760 | tf_op jit(solution)/shard_map/all_to_all | solution.py:79
  133.2 4.6 %copy.44 = bf16[2048,640]{0,1:T(8,128)(2,1)} copy(bf16[2048,640]{1,0:T(8,128)(2,1)} %param.16) | data formatting | bytes 5242880 | tf_op args[3]
  137.8 0.5 multiply_reduce_fusion
  138.3 3.4 fusion.45
  141.7 1.0 copy-done.4
  142.8 0.8 slice.176
  143.6 1.2 multiply_reduce_fusion.2
  144.9 2.4 multiply_reduce_fusion.1
  148.7 0.6 fusion.89
  149.3 1.3 iota_compare_fusion.2
  150.7 0.6 fusion.17
  151.3 96.6 %all-to-all-done.1 = bf16[16,5,256,128]{3,2,1,0:T(8,128)(2,1)} async-done(((bf16[16,5,256,128]{3,2,1,0:T(8,128)(2,1)}), bf16[16,5,256,128]{3,2,1,0:T(8,128)(2,1)}, u32[]{:S(2)}, u32[]{:S(2)}) %all-to-all-start.1) | async-done | bytes 5242912 | tf_op jit(solution)/shard_map/all_to_all | solution.py:79
  247.9 2.8 copy.43
  250.7 1.2 bitcast_select_fusion
  252.0 4.1 %fusion.14 = (bf16[5,2304,128]{2,1,0:T(8,128)(2,1)}, bf16[5,2304,128]{2,1,0:T(8,128)(2,1)}) fusion(bf16[2,5,2048,128]{3,2,1,0:T(8,128)(2,1)S(1)} %bitcast_select_fusion, bf16[2,5,256,128]{3,2,1,0:T(8,128)(2,1)S(1)} %copy.45), kind=kLoop, calls=%fused_computation.33 | loop fusion | flops 11796480 | bytes 11796480 | tf_op jit(solution)/shard_map/squeeze | solution.py:119
  256.1 4.6 %gather_fusion.1 = bf16[5,2304,128]{2,1,0:T(8,128)(2,1)} fusion(bf16[5,2304,128]{2,1,0:T(8,128)(2,1)} %get-tuple-element.49, s32[1024]{0:T(1024)S(1)} %pad_clamp_fusion), kind=kCustom, calls=%fused_computation.clone | custom fusion | bytes 5898260 | tf_op jit(solution)/shard_map/jit(_take)/gather | solution.py:119
  260.7 5.4 %copy.46 = bf16[5,2304,128]{1,2,0:T(8,128)(2,1)} copy(bf16[5,2304,128]{2,1,0:T(8,128)(2,1)} %gather_fusion.1) | data formatting | bytes 5898240 | tf_op jit(solution)/shard_map/jit(_take)/gather | solution.py:119
  266.1 4.6 %gather_fusion.2 = bf16[5,2304,128]{2,1,0:T(8,128)(2,1)} fusion(bf16[5,2304,128]{2,1,0:T(8,128)(2,1)} %get-tuple-element.50, s32[1024]{0:T(1024)S(1)} %pad_clamp_fusion), kind=kCustom, calls=%fused_computation.1.clone | custom fusion | bytes 5898260 | tf_op jit(solution)/shard_map/jit(_take)/gather | solution.py:119
  270.8 5.4 %copy.47 = bf16[5,2304,128]{1,2,0:T(8,128)(2,1)} copy(bf16[5,2304,128]{2,1,0:T(8,128)(2,1)} %gather_fusion.2) | data formatting | bytes 5898240 | tf_op jit(solution)/shard_map/jit(_take)/gather | solution.py:119
  276.2 5.8 %broadcast_select_fusion.1 = (bf16[5,2304,128]{1,2,0:T(8,128)(2,1)}, bf16[5,2304,128]{1,2,0:T(8,128)(2,1)}) fusion(bf16[5,2304,128]{1,2,0:T(8,128)(2,1)} %copy.46, pred[5]{0:T(512)(128)(4,1)S(1)} %compare_and_fusion, bf16[5,2304,128]{1,2,0:T(8,128)(2,1)} %copy.47), kind=kLoop, calls=%fused_computation.37 | loop fusion | flops 2949120 | bytes 11796485 | tf_op jit(solution)/shard_map/jit(_take)/select_n | solution.py:119
  282.0 5.2 %fusion.90 = f32[5,256]{1,0:T(8,128)S(1)} fusion(pred[256,2304]{1,0:T(8,128)(4,1)S(1)} %get-tuple-element.58, bf16[5,2304,128]{1,2,0:T(8,128)(2,1)} %get-tuple-element.62, bf16[2,256,5,32]{1,3,2,0:T(8,128)(2,1)S(1)} %get-tuple-element.52, bf16[2,256,5,32]{1,3,2,0:T(8,128)(2,1)S(1)} %get-tuple-element.51), kind=kOutput, calls=%fused_computation.119 | convolution fusion | flops 389613824 | bytes 2397184 | tf_op jit(solution)/shard_map/sub | solution.py:43
  287.2 7.0 %fusion.37 = bf16[5,64,256]{2,1,0:T(8,128)(2,1)} fusion(f32[5,256]{1,0:T(8,128)S(1)} %fusion.90, bf16[5,2304,128]{1,2,0:T(8,128)(2,1)} %get-tuple-element.62, pred[256,2304]{1,0:T(8,128)(4,1)S(1)} %get-tuple-element.58, bf16[2,256,5,32]{1,3,2,0:T(8,128)(2,1)S(1)} %get-tuple-element.52, bf16[2,256,5,32]{1,3,2,0:T(8,128)(2,1)S(1)} %get-tuple-element.51), kind=kOutput, calls=%fused_computation.54 | convolution fusion | flops 770133504 | bytes 4035584 | tf_op jit(solution)/shard_map/hqk,hkd->qhd/dot_general | solution.py:45
  294.2 5.5 %fusion.95 = f32[5,256]{1,0:T(8,128)S(1)} fusion(pred[256,2304]{1,0:T(8,128)(4,1)S(1)} %get-tuple-element.57, bf16[5,2304,128]{1,2,0:T(8,128)(2,1)} %get-tuple-element.61, bf16[2,256,5,32]{1,3,2,0:T(8,128)(2,1)S(1)} %get-tuple-element.51, bf16[2,256,5,32]{1,3,2,0:T(8,128)(2,1)S(1)} %get-tuple-element.52), kind=kOutput, calls=%fused_computation.120 | convolution fusion | flops 389613824 | bytes 2397184 | tf_op jit(solution)/shard_map/sub | solution.py:43
  299.6 6.3 %fusion.40 = bf16[5,64,256]{2,1,0:T(8,128)(2,1)S(1)} fusion(f32[5,256]{1,0:T(8,128)S(1)} %fusion.95, bf16[5,2304,128]{1,2,0:T(8,128)(2,1)} %get-tuple-element.61, pred[256,2304]{1,0:T(8,128)(4,1)S(1)} %get-tuple-element.57, bf16[2,256,5,32]{1,3,2,0:T(8,128)(2,1)S(1)} %get-tuple-element.51, bf16[2,256,5,32]{1,3,2,0:T(8,128)(2,1)S(1)} %get-tuple-element.52), kind=kOutput, calls=%fused_computation.55 | convolution fusion | flops 770133504 | bytes 4035584 | tf_op jit(solution)/shard_map/hqk,hkd->qhd/dot_general | solution.py:45
  306.0 3.3 fusion.47
  309.3 0.6 copy-done.14
  310.1 5.6 %concatenate.30 = bf16[2,5,2304,128]{3,2,1,0:T(8,128)(2,1)} pad(bf16[2,5,2048,128]{3,2,1,0:T(8,128)(2,1)} %copy-done.1, bf16[]{:T(256)} %constant.52.clone.1), padding=0_0x0_0x0_256x0_0 | pad | bytes 11141122 | tf_op jit(solution)/shard_map/concatenate | solution.py:131
  315.7 24.9 %while.1 = (s32[]{:T(128)}, bf16[2,5,2304,128]{3,2,1,0:T(8,128)(2,1)}, s32[2,4]{1,0:T(2,128)S(1)}, bf16[2,5,256,128]{3,2,1,0:T(8,128)(2,1)S(1)}, s32[]{:T(128)}, /*index=5*/s32[4]{0:T(128)S(1)}, s32[]{:T(128)}) while((s32[]{:T(128)}, bf16[2,5,2304,128]{3,2,1,0:T(8,128)(2,1)}, s32[2,4]{1,0:T(2,128)S(1)}, bf16[2,5,256,128]{3,2,1,0:T(8,128)(2,1)S(1)}, ...), condition=%wide.while_cond, body=%wide.while_body.sunk | while | flops 163869 | bytes 1638603 | solution.py:136
  315.7 0.6 fusion.104
  316.3 3.2 and_reduce_fusion.2
  319.5 3.0 dynamic-slice_select_fusion.2
  322.5 5.6 %dynamic-update-slice.3 = bf16[2,5,2304,128]{3,2,1,0:T(8,128)(2,1)} dynamic-update-slice(bf16[2,5,2304,128]{3,2,1,0:T(8,128)(2,1)} %get-tuple-element.113, bf16[1,5,256,128]{3,2,1,0:T(8,128)(2,1)S(1)} %dynamic-slice_select_fusion.2, s32[]{:T(128)} %bitcast.89, s32[]{:T(128)} %constant.38.clone.1..sunk, s32[]{:T(128)} %bitcast.90, s32[]{:T(128)} %constant.38.clone.1..sunk) | dynamic-update-slice | bytes 655364 | tf_op jit(solution)/shard_map/vmap(vmap())/scatter
  328.1 0.6 fusion.104
  328.7 3.2 and_reduce_fusion.2
  332.0 3.0 dynamic-slice_select_fusion.2
  335.0 5.6 %dynamic-update-slice.3 = bf16[2,5,2304,128]{3,2,1,0:T(8,128)(2,1)} dynamic-update-slice(bf16[2,5,2304,128]{3,2,1,0:T(8,128)(2,1)} %get-tuple-element.113, bf16[1,5,256,128]{3,2,1,0:T(8,128)(2,1)S(1)} %dynamic-slice_select_fusion.2, s32[]{:T(128)} %bitcast.89, s32[]{:T(128)} %constant.38.clone.1..sunk, s32[]{:T(128)} %bitcast.90, s32[]{:T(128)} %constant.38.clone.1..sunk) | dynamic-update-slice | bytes 655364 | tf_op jit(solution)/shard_map/vmap(vmap())/scatter
  340.5 2.7 constant_dynamic-slice_fusion.2
  343.3 1.7 collective-permute-start
  344.9 15.9 %collective-permute-done = bf16[2,5,288,128]{3,2,1,0:T(8,128)(2,1)} collective-permute-done((bf16[2,5,288,128]{3,2,1,0:T(8,128)(2,1)}, bf16[2,5,288,128]{3,2,1,0:T(8,128)(2,1)}, u32[]{:S(2)}, u32[]{:S(2)}) %collective-permute-start) | collective-permute-done | bytes 737312 | tf_op jit(solution)/shard_map/ppermute | solution.py:11
  360.8 3.2 maximum_select_fusion
  364.0 30.0 %all-reduce.3.cloned.1.call-done = f32[512,2048]{1,0:T(8,128)} async-done(((f32[512,2048]{1,0:T(8,128)}), f32[512,2048]{1,0:T(8,128)}) %all-reduce.3.cloned.1.call-update) | async-done | bytes 4194320 | tf_op jit(solution)/shard_map/psum | solution.py:128
  394.0 4.2 %fusion.12 = bf16[512,2048]{1,0:T(8,128)(2,1)} fusion(f32[512,2048]{1,0:T(8,128)} %all-reduce.3.cloned.1.call-done, bf16[2,256,2048]{2,1,0:T(8,128)(2,1)S(1)} %copy-done.3), kind=kLoop, calls=%fused_computation.29 | loop fusion | flops 3145728 | bytes 8388608 | tf_op jit(solution)/shard_map/convert_element_type | solution.py:129
  (58 shorter events, 2.1 us)
Async XLA Ops:
  7.2 298.8 %copy-start = (bf16[320,2048]{1,0:T(8,128)(2,1)S(1)}, bf16[320,2048]{1,0:T(8,128)(2,1)}, u32[]{:S(2)}) copy-start(bf16[320,2048]{1,0:T(8,128)(2,1)} %param.17) | copy-start | bytes 3932164
  12.4 7.4 %copy-start.9 = (s32[16]{0:T(128)S(1)}, s32[16]{0:T(128)}, u32[]{:S(2)}) copy-start(s32[16]{0:T(128)} %param.21) | copy-start | bytes 196
  12.4 7.4 %copy-start.12 = (s32[16]{0:T(128)S(1)}, s32[16]{0:T(128)}, u32[]{:S(2)}) copy-start(s32[16]{0:T(128)} %param.22) | copy-start | bytes 196
  12.4 100.7 %all-to-all-start = ((bf16[1,5,2048,128]{3,1,0,2:T(8,128)(2,1)}), bf16[1,5,2048,128]{3,1,0,2:T(8,128)(2,1)}, u32[]{:S(2)}, u32[]{:S(2)}) async-start(bf16[1,5,2048,128]{3,1,0,2:T(8,128)(2,1)} %copy.40), calls=%async_computation | async-start | bytes 8388608 | tf_op jit(solution)/shard_map/all_to_all | solution.py:75
  128.3 119.6 %all-to-all-start.1 = ((bf16[16,5,256,128]{3,2,1,0:T(8,128)(2,1)}), bf16[16,5,256,128]{3,2,1,0:T(8,128)(2,1)}, u32[]{:S(2)}, u32[]{:S(2)}) async-start(bf16[16,5,256,128]{3,2,1,0:T(8,128)(2,1)} %select_select_fusion), calls=%async_computation.1 | async-start | bytes 10485760 | tf_op jit(solution)/shard_map/all_to_all | solution.py:79
  133.0 4.8 %copy-start.2 = (bf16[2,256,2048]{2,1,0:T(8,128)(2,1)S(1)}, bf16[2,256,2048]{2,1,0:T(8,128)(2,1)}, u32[]{:S(2)}) copy-start(bf16[2,256,2048]{2,1,0:T(8,128)(2,1)} %param.13) | copy-start | bytes 6291460
  133.0 261.0 %all-reduce.3.cloned.1.call-start = ((), (), s32[]{:S(2)}) async-start(), calls=%async_computation.2 | async-start | bytes 8388608 | tf_op jit(solution)/shard_map/psum | solution.py:128
  133.2 5.1 %copy-start.15 = (f32[2048]{0:T(1024)S(1)}, f32[2048]{0:T(1024)}, u32[]{:S(2)}) copy-start(f32[2048]{0:T(1024)} %param.14) | copy-start | bytes 24580
  138.3 5.2 %copy-start.13 = (s32[16]{0:T(128)S(1)}, s32[16]{0:T(128)}, u32[]{:S(2)}) copy-start(s32[16]{0:T(128)} %param.23) | copy-start | bytes 196
  141.7 1.1 copy-start.4
  144.9 2.8 copy-start.5
  144.9 2.8 copy-start.10
  144.9 2.8 copy-start.11
  147.3 1.0 copy-start.6
  252.0 4.1 %copy-start.1 = (bf16[2,5,2048,128]{3,2,1,0:T(8,128)(2,1)}, bf16[2,5,2048,128]{3,2,1,0:T(8,128)(2,1)S(1)}, u32[]{:S(2)}) copy-start(bf16[2,5,2048,128]{3,2,1,0:T(8,128)(2,1)S(1)} %bitcast_select_fusion) | copy-start | bytes 15728644
  299.6 6.4 %copy-start.7 = (bf16[5,64,256]{2,1,0:T(8,128)(2,1)S(1)}, bf16[5,64,256]{2,1,0:T(8,128)(2,1)}, u32[]{:S(2)}) copy-start(bf16[5,64,256]{2,1,0:T(8,128)(2,1)} %fusion.37) | copy-start | bytes 491524
  309.3 0.7 copy-start.14
  310.1 5.6 %copy-start.8 = (s32[4]{0:T(128)S(1)}, s32[4]{0:T(128)}, u32[]{:S(2)}) copy-start(s32[4]{0:T(128)} %constant.238) | copy-start | bytes 52
  340.5 53.4 %copy-start.3 = (bf16[2,256,2048]{2,1,0:T(8,128)(2,1)S(1)}, bf16[2,256,2048]{2,1,0:T(8,128)(2,1)}, u32[]{:S(2)}) copy-start(bf16[2,256,2048]{2,1,0:T(8,128)(2,1)} %param.13) | copy-start | bytes 6291460
  343.3 17.6 %collective-permute-start = (bf16[2,5,288,128]{3,2,1,0:T(8,128)(2,1)}, bf16[2,5,288,128]{3,2,1,0:T(8,128)(2,1)}, u32[]{:S(2)}, u32[]{:S(2)}) collective-permute-start(bf16[2,5,288,128]{3,2,1,0:T(8,128)(2,1)} %get-tuple-element.48), channel_id=1, source_target_pairs={{0,4},{4,0},{8,12},{12,8},{16,20},{20,16},{24,28},{28,24},{1,5},{5... | collective-permute-start | bytes 2211848 | tf_op jit(solution)/shard_map/ppermute | solution.py:11
Sparse Core Ops, SparseCore 0:
  309.4 84.5 all-reduce.2
where the time goes:
time: 407 us; the launch traced here: 405 us
  waiting for transfers between devices  236 us (58%)
  local copies, waits for them, and re-layouts  66.8 us (16%)
  other arithmetic  41.1 us (10%)
  matrix products  33 us (8%)
  between operations  14.3 us (4%)
  starting transfers between devices  13.9 us (3%)
    all_to_all x1, waiting for transfers between devices, on_device(): lax.all_to_all(jnp.where(live_all[:, None, None, None], select_chosen, jn...  96.6 us
    all_to_all x1, waiting for transfers between devices, on_device(): lax.all_to_all(stored, 'req', split_axis=2, concat_axis=0, tiled=True)  93.2 us
    psum x1, waiting for transfers between devices, on_device(): lax.psum(jnp.dot(mixed_all, w_out, preferred_element_type=jnp.float32), '...  30 us
    gather x4, local copies, waits for them, and re-layouts, on_device(): chosen = jnp.take(keys_all[number], head_select, axis=0)  20.1 us
    ppermute x1, waiting for transfers between devices, swapped(): return lax.ppermute(value, axis, pairs)  15.9 us
    dot_general x2, matrix products, attend(): jnp.einsum('hqk,hkd->qhd', probs, keys_one[..., head_dim:], preferred_ele...  13.3 us
    scatter x6, local copies, waits for them, and re-layouts  12.4 us
    scatter x4, other arithmetic  12.4 us
  transfers between devices with their start and end apart: 4, of which 4 were waited for; matrix products, arithmetic and copies ran while one was open for 13% of the time, Pallas kernels for 0%

commit v1 on v0

--- a/solution.py
+++ b/solution.py
@@ -3,6 +3,22 @@
 import jax.numpy as jnp
 from jax import lax
 from jax.sharding import PartitionSpec as P
+
+
+def exchange_in_pairs(value, axis, split, join):
+    ways, here = (lax.axis_size(axis), lax.axis_index(axis))
+    width = value.shape[split] // ways
+    lengths = list(value.shape)
+    lengths[split] = width
+    height = lengths[join]
+    lengths[join] = height * ways
+    full = jnp.zeros(lengths, value.dtype)
+    for mask in range(ways):
+        part = lax.dynamic_slice_in_dim(value, (here ^ mask) * width, width, axis=split)
+        if mask:
+            part = lax.ppermute(part, axis, [(d, d ^ mask) for d in range(ways)])
+        full = lax.dynamic_update_slice_in_dim(full, part, (here ^ mask) * height, axis=join)
+    return full
 
 
 def swapped(value, axis, apart):
@@ -72,7 +88,7 @@
     cache_span = stored.shape[2]
     total_length = cache_span + new_count
     scale = 1.0 / math.sqrt(head_dim)
-    relayed = lax.all_to_all(stored, "req", split_axis=2, concat_axis=0, tiled=True)
+    relayed = exchange_in_pairs(stored, "req", 2, 0)
     live_all = continuing == 1
     rows_all = jnp.where(live_all, cache_row, 0)
     select_chosen = jnp.take(relayed, rows_all, axis=0)

time: 407 us -> 364 us (0.89)
  waiting for transfers between devices: 236 us -> 175 us
  starting transfers between devices: 13.9 us -> 27.6 us
  local copies, waits for them, and re-layouts: 66.8 us -> 71.1 us
    all_to_all x1 -> x0, waiting for transfers between devices: 93.2 us -> none  [on_device(): lax.all_to_all(stored, 'req', split_axis=2, concat_axis=0, tiled=True)]
    ppermute x0 -> x7, waiting for transfers between devices: none -> 32 us  [exchange_in_pairs(): part = lax.ppermute(part, axis, [(d, d ^ mask) for d in range(ways)])]
    ppermute x0 -> x7, starting transfers between devices: none -> 13.6 us  [exchange_in_pairs(): part = lax.ppermute(part, axis, [(d, d ^ mask) for d in range(ways)])]
    dynamic_update_slice x0 -> x7, local copies, waits for them, and re-layouts: none -> 10.1 us  [exchange_in_pairs(): lax.dynamic_update_slice_in_dim(full, part, (here ^ mask) * height, axis=...]
    all_to_all x1, starting transfers between devices: 4.65 us -> 13.5 us  [on_device(): lax.all_to_all(jnp.where(live_all[:, None, None, None], select_chosen, jn...]
    all_to_all x1 -> x0, starting transfers between devices: 7.41 us -> none  [on_device(): lax.all_to_all(stored, 'req', split_axis=2, concat_axis=0, tiled=True)]
    unnamed x36 -> x37, local copies, waits for them, and re-layouts: 11.8 us -> 6.92 us
    all_to_all x1 -> x0, local copies, waits for them, and re-layouts: 4.45 us -> none  [on_device(): lax.all_to_all(stored, 'req', split_axis=2, concat_axis=0, tiled=True)]
  transfers between devices with their start and end apart: 4 -> 10, of which waited for: 4 -> 7; matrix products, arithmetic and copies ran while one was open for 13% -> 17% of each run, Pallas kernels for 0% -> 0%
where the time goes in v1:
time: 364 us; the launch traced here: 362 us
  waiting for transfers between devices  175 us (48%)
  local copies, waits for them, and re-layouts  71.1 us (20%)
  other arithmetic  41.2 us (11%)
  matrix products  32.9 us (9%)
  starting transfers between devices  27.6 us (8%)
  between operations  14.4 us (4%)
    all_to_all x1, waiting for transfers between devices, on_device(): lax.all_to_all(jnp.where(live_all[:, None, None, None], select_chosen, jn...  97.1 us
    ppermute x7, waiting for transfers between devices, exchange_in_pairs(): part = lax.ppermute(part, axis, [(d, d ^ mask) for d in range(ways)])  32 us
    psum x1, waiting for transfers between devices, on_device(): lax.psum(jnp.dot(mixed_all, w_out, preferred_element_type=jnp.float32), '...  29.6 us
    gather x4, local copies, waits for them, and re-layouts, on_device(): chosen = jnp.take(keys_all[number], head_select, axis=0)  20.1 us
    ppermute x1, waiting for transfers between devices, swapped(): return lax.ppermute(value, axis, pairs)  15.9 us
    ppermute x7, starting transfers between devices, exchange_in_pairs(): part = lax.ppermute(part, axis, [(d, d ^ mask) for d in range(ways)])  13.6 us
    all_to_all x1, starting transfers between devices, on_device(): lax.all_to_all(jnp.where(live_all[:, None, None, None], select_chosen, jn...  13.5 us
    dot_general x2, matrix products, attend(): jnp.einsum('hqk,hkd->qhd', probs, keys_one[..., head_dim:], preferred_ele...  13.3 us
  transfers between devices with their start and end apart: 10, of which 7 were waited for; matrix products, arithmetic and copies ran while one was open for 17% of the time, Pallas kernels for 0%

profile of v1, /device:TPU:0, one launch (start us, length us, event | category | flops | bytes accessed | tf_op | source)
XLA Modules:
  0.0 361.9 jit_solution(6974599988811653636)
XLA Ops:
  7.2 2.1 broadcast_in_dim.138
  10.7 3.0 collective-permute-start
  13.7 1.6 collective-permute-start.1
  15.3 3.0 collective-permute-start.3
  18.2 1.3 collective-permute-start.4
  19.6 2.1 collective-permute-done
  21.7 3.8 %collective-permute-start.5 = (bf16[1,5,256,128]{3,2,1,0:T(8,128)(2,1)S(1)}, bf16[1,5,256,128]{3,2,1,0:T(8,128)(2,1)S(1)}, u32[]{:S(2)}, u32[]{:S(2)}) collective-permute-start(bf16[1,5,256,128]{3,2,1,0:T(8,128)(2,1)S(1)} %get-tuple-element.46), channel_id=1, source_target_pairs={{0,24},{4,28},{8,16},{12,20},{16,8},{20,12},{24,0},{28,4},{1,25},{... | collective-permute-start | bytes 983048 | tf_op jit(solution)/shard_map/ppermute | solution.py:19
  25.5 1.7 constant_dynamic-update-slice_fusion.6
  27.2 10.3 %collective-permute-done.1 = bf16[1,5,256,128]{3,2,1,0:T(8,128)(2,1)} collective-permute-done((bf16[1,5,256,128]{3,2,1,0:T(8,128)(2,1)S(1)}, bf16[1,5,256,128]{3,2,1,0:T(8,128)(2,1)}, u32[]{:S(2)}, u32[]{:S(2)}) %collective-permute-start.1) | collective-permute-done | bytes 327712 | tf_op jit(solution)/shard_map/ppermute | solution.py:19
  38.5 1.7 constant_dynamic-update-slice_fusion.5
  40.2 1.9 collective-permute-done.2
  42.2 1.7 constant_dynamic-update-slice_fusion.4
  43.9 1.7 constant_dynamic-update-slice_fusion.3
  45.6 17.7 %collective-permute-done.4 = bf16[1,5,256,128]{3,2,1,0:T(8,128)(2,1)} collective-permute-done((bf16[1,5,256,128]{3,2,1,0:T(8,128)(2,1)S(1)}, bf16[1,5,256,128]{3,2,1,0:T(8,128)(2,1)}, u32[]{:S(2)}, u32[]{:S(2)}) %collective-permute-start.4) | collective-permute-done | bytes 327712 | tf_op jit(solution)/shard_map/ppermute | solution.py:19
  63.4 1.7 constant_dynamic-update-slice_fusion.2
  66.6 5.3 %gather_fusion = bf16[16,5,256,128]{3,2,1,0:T(8,128)(2,1)} fusion(bf16[8,5,256,128]{3,2,1,0:T(8,128)(2,1)} %constant_dynamic-update-slice_fusion, s32[1024]{0:T(1024)S(1)} %pad_clamp_fusion.1), kind=kCustom, calls=%fused_computation.2 | custom fusion | bytes 10485824 | tf_op jit(solution)/shard_map/jit(_take)/gather | solution.py:94
  71.9 5.5 %select_select_fusion = bf16[16,5,256,128]{3,2,1,0:T(8,128)(2,1)} fusion(bf16[16,5,256,128]{3,2,1,0:T(8,128)(2,1)} %gather_fusion, pred[16]{0:T(512)(128)(4,1)S(1)} %get-tuple-element.29, pred[16]{0:T(512)(128)(4,1)S(1)} %get-tuple-element.61), kind=kLoop, calls=%fused_computation.27 | loop fusion | flops 5242880 | bytes 10485792 | tf_op jit(solution)/shard_map/jit(_where)/select_n | solution.py:96
  77.3 13.5 %all-to-all-start = ((bf16[16,5,256,128]{3,2,1,0:T(8,128)(2,1)}), bf16[16,5,256,128]{3,2,1,0:T(8,128)(2,1)}, u32[]{:S(2)}, u32[]{:S(2)}) async-start(bf16[16,5,256,128]{3,2,1,0:T(8,128)(2,1)} %select_select_fusion), calls=%async_computation | async-start | bytes 10485760 | tf_op jit(solution)/shard_map/all_to_all | solution.py:95
  90.9 4.6 %copy.18 = bf16[2048,640]{0,1:T(8,128)(2,1)} copy(bf16[2048,640]{1,0:T(8,128)(2,1)} %param.16) | data formatting | bytes 5242880 | tf_op args[3]
  96.0 3.4 fusion.45
  102.6 2.4 multiply_reduce_fusion.1
  107.0 1.3 iota_compare_fusion.2
  109.0 97.1 %all-to-all-done = bf16[16,5,256,128]{3,2,1,0:T(8,128)(2,1)} async-done(((bf16[16,5,256,128]{3,2,1,0:T(8,128)(2,1)}), bf16[16,5,256,128]{3,2,1,0:T(8,128)(2,1)}, u32[]{:S(2)}, u32[]{:S(2)}) %all-to-all-start) | async-done | bytes 5242912 | tf_op jit(solution)/shard_map/all_to_all | solution.py:95
  206.1 2.8 copy.17
  210.1 4.1 %fusion.14 = (bf16[5,2304,128]{2,1,0:T(8,128)(2,1)}, bf16[5,2304,128]{2,1,0:T(8,128)(2,1)}) fusion(bf16[2,5,2048,128]{3,2,1,0:T(8,128)(2,1)S(1)} %bitcast_select_fusion, bf16[2,5,256,128]{3,2,1,0:T(8,128)(2,1)S(1)} %copy.19), kind=kLoop, calls=%fused_computation.33 | loop fusion | flops 11796480 | bytes 11796480 | tf_op jit(solution)/shard_map/squeeze | solution.py:135
  214.3 4.6 %gather_fusion.1 = bf16[5,2304,128]{2,1,0:T(8,128)(2,1)} fusion(bf16[5,2304,128]{2,1,0:T(8,128)(2,1)} %get-tuple-element.37, s32[1024]{0:T(1024)S(1)} %pad_clamp_fusion), kind=kCustom, calls=%fused_computation.clone | custom fusion | bytes 5898260 | tf_op jit(solution)/shard_map/jit(_take)/gather | solution.py:135
  218.9 5.4 %copy.20 = bf16[5,2304,128]{1,2,0:T(8,128)(2,1)} copy(bf16[5,2304,128]{2,1,0:T(8,128)(2,1)} %gather_fusion.1) | data formatting | bytes 5898240 | tf_op jit(solution)/shard_map/jit(_take)/gather | solution.py:135
  224.3 4.6 %gather_fusion.2 = bf16[5,2304,128]{2,1,0:T(8,128)(2,1)} fusion(bf16[5,2304,128]{2,1,0:T(8,128)(2,1)} %get-tuple-element.38, s32[1024]{0:T(1024)S(1)} %pad_clamp_fusion), kind=kCustom, calls=%fused_computation.1.clone | custom fusion | bytes 5898260 | tf_op jit(solution)/shard_map/jit(_take)/gather | solution.py:135
  228.9 5.4 %copy.21 = bf16[5,2304,128]{1,2,0:T(8,128)(2,1)} copy(bf16[5,2304,128]{2,1,0:T(8,128)(2,1)} %gather_fusion.2) | data formatting | bytes 5898240 | tf_op jit(solution)/shard_map/jit(_take)/gather | solution.py:135
  234.3 5.9 %broadcast_select_fusion.1 = (bf16[5,2304,128]{1,2,0:T(8,128)(2,1)}, bf16[5,2304,128]{1,2,0:T(8,128)(2,1)}) fusion(bf16[5,2304,128]{1,2,0:T(8,128)(2,1)} %copy.20, pred[5]{0:T(512)(128)(4,1)S(1)} %compare_and_fusion, bf16[5,2304,128]{1,2,0:T(8,128)(2,1)} %copy.21), kind=kLoop, calls=%fused_computation.37 | loop fusion | flops 2949120 | bytes 11796485 | tf_op jit(solution)/shard_map/jit(_take)/select_n | solution.py:135
  240.2 5.2 %fusion.90 = f32[5,256]{1,0:T(8,128)S(1)} fusion(pred[256,2304]{1,0:T(8,128)(4,1)S(1)} %get-tuple-element.54, bf16[5,2304,128]{1,2,0:T(8,128)(2,1)} %get-tuple-element.58, bf16[2,256,5,32]{1,3,2,0:T(8,128)(2,1)S(1)} %get-tuple-element.48, bf16[2,256,5,32]{1,3,2,0:T(8,128)(2,1)S(1)} %get-tuple-element.47), kind=kOutput, calls=%fused_computation.133 | convolution fusion | flops 389613824 | bytes 2397184 | tf_op jit(solution)/shard_map/sub | solution.py:59
  245.4 7.0 %fusion.37 = bf16[5,64,256]{2,1,0:T(8,128)(2,1)} fusion(f32[5,256]{1,0:T(8,128)S(1)} %fusion.90, bf16[5,2304,128]{1,2,0:T(8,128)(2,1)} %get-tuple-element.58, pred[256,2304]{1,0:T(8,128)(4,1)S(1)} %get-tuple-element.54, bf16[2,256,5,32]{1,3,2,0:T(8,128)(2,1)S(1)} %get-tuple-element.48, bf16[2,256,5,32]{1,3,2,0:T(8,128)(2,1)S(1)} %get-tuple-element.47), kind=kOutput, calls=%fused_computation.53 | convolution fusion | flops 770133504 | bytes 4035584 | tf_op jit(solution)/shard_map/hqk,hkd->qhd/dot_general | solution.py:61
  252.4 5.4 %fusion.95 = f32[5,256]{1,0:T(8,128)S(1)} fusion(pred[256,2304]{1,0:T(8,128)(4,1)S(1)} %get-tuple-element.53, bf16[5,2304,128]{1,2,0:T(8,128)(2,1)} %get-tuple-element.57, bf16[2,256,5,32]{1,3,2,0:T(8,128)(2,1)S(1)} %get-tuple-element.47, bf16[2,256,5,32]{1,3,2,0:T(8,128)(2,1)S(1)} %get-tuple-element.48), kind=kOutput, calls=%fused_computation.134 | convolution fusion | flops 389613824 | bytes 2397184 | tf_op jit(solution)/shard_map/sub | solution.py:59
  257.8 6.3 %fusion.40 = bf16[5,64,256]{2,1,0:T(8,128)(2,1)S(1)} fusion(f32[5,256]{1,0:T(8,128)S(1)} %fusion.95, bf16[5,2304,128]{1,2,0:T(8,128)(2,1)} %get-tuple-element.57, pred[256,2304]{1,0:T(8,128)(4,1)S(1)} %get-tuple-element.53, bf16[2,256,5,32]{1,3,2,0:T(8,128)(2,1)S(1)} %get-tuple-element.47, bf16[2,256,5,32]{1,3,2,0:T(8,128)(2,1)S(1)} %get-tuple-element.48), kind=kOutput, calls=%fused_computation.54 | convolution fusion | flops 770133504 | bytes 4035584 | tf_op jit(solution)/shard_map/hqk,hkd->qhd/dot_general | solution.py:61
  264.2 3.2 fusion.47
  268.2 5.6 %concatenate.30 = bf16[2,5,2304,128]{3,2,1,0:T(8,128)(2,1)} pad(bf16[2,5,2048,128]{3,2,1,0:T(8,128)(2,1)} %copy-done.1, bf16[]{:T(256)} %constant.35.clone.1), padding=0_0x0_0x0_256x0_0 | pad | bytes 11141122 | tf_op jit(solution)/shard_map/concatenate | solution.py:147
  273.9 25.3 %while.1 = (s32[]{:T(128)}, bf16[2,5,2304,128]{3,2,1,0:T(8,128)(2,1)}, s32[2,4]{1,0:T(2,128)S(1)}, bf16[2,5,256,128]{3,2,1,0:T(8,128)(2,1)S(1)}, s32[]{:T(128)}, /*index=5*/s32[4]{0:T(128)S(1)}, s32[]{:T(128)}) while((s32[]{:T(128)}, bf16[2,5,2304,128]{3,2,1,0:T(8,128)(2,1)}, s32[2,4]{1,0:T(2,128)S(1)}, bf16[2,5,256,128]{3,2,1,0:T(8,128)(2,1)S(1)}, ...), condition=%wide.while_cond, body=%wide.while_body.sunk | while | flops 163869 | bytes 1638603 | solution.py:152
  274.5 3.2 and_reduce_fusion.2
  277.8 3.0 dynamic-slice_select_fusion.2
  280.8 5.7 %dynamic-update-slice.3 = bf16[2,5,2304,128]{3,2,1,0:T(8,128)(2,1)} dynamic-update-slice(bf16[2,5,2304,128]{3,2,1,0:T(8,128)(2,1)} %get-tuple-element.109, bf16[1,5,256,128]{3,2,1,0:T(8,128)(2,1)S(1)} %dynamic-slice_select_fusion.2, s32[]{:T(128)} %bitcast.83, s32[]{:T(128)} %constant.41.clone.1..sunk, s32[]{:T(128)} %bitcast.84, s32[]{:T(128)} %constant.41.clone.1..sunk) | dynamic-update-slice | bytes 655364 | tf_op jit(solution)/shard_map/vmap(vmap())/scatter
  287.2 3.2 and_reduce_fusion.2
  290.4 3.0 dynamic-slice_select_fusion.2
  293.4 5.7 %dynamic-update-slice.3 = bf16[2,5,2304,128]{3,2,1,0:T(8,128)(2,1)} dynamic-update-slice(bf16[2,5,2304,128]{3,2,1,0:T(8,128)(2,1)} %get-tuple-element.109, bf16[1,5,256,128]{3,2,1,0:T(8,128)(2,1)S(1)} %dynamic-slice_select_fusion.2, s32[]{:T(128)} %bitcast.83, s32[]{:T(128)} %constant.41.clone.1..sunk, s32[]{:T(128)} %bitcast.84, s32[]{:T(128)} %constant.41.clone.1..sunk) | dynamic-update-slice | bytes 655364 | tf_op jit(solution)/shard_map/vmap(vmap())/scatter
  299.1 2.7 constant_dynamic-slice_fusion.2
  302.3 15.9 %collective-permute-done.7 = bf16[2,5,288,128]{3,2,1,0:T(8,128)(2,1)} collective-permute-done((bf16[2,5,288,128]{3,2,1,0:T(8,128)(2,1)}, bf16[2,5,288,128]{3,2,1,0:T(8,128)(2,1)}, u32[]{:S(2)}, u32[]{:S(2)}) %collective-permute-start.7) | collective-permute-done | bytes 737312 | tf_op jit(solution)/shard_map/ppermute | solution.py:27
  318.2 3.1 maximum_select_fusion
  321.3 29.6 %all-reduce.3.cloned.1.call-done = f32[512,2048]{1,0:T(8,128)} async-done(((f32[512,2048]{1,0:T(8,128)}), f32[512,2048]{1,0:T(8,128)}) %all-reduce.3.cloned.1.call-update) | async-done | bytes 4194320 | tf_op jit(solution)/shard_map/psum | solution.py:144
  350.9 4.2 %fusion.12 = bf16[512,2048]{1,0:T(8,128)(2,1)} fusion(f32[512,2048]{1,0:T(8,128)} %all-reduce.3.cloned.1.call-done, bf16[2,256,2048]{2,1,0:T(8,128)(2,1)S(1)} %copy-done.3), kind=kLoop, calls=%fused_computation.29 | loop fusion | flops 3145728 | bytes 8388608 | tf_op jit(solution)/shard_map/convert_element_type | solution.py:145
  (79 shorter events, 14.0 us)
Async XLA Ops:
  7.2 257.0 %copy-start = (bf16[320,2048]{1,0:T(8,128)(2,1)S(1)}, bf16[320,2048]{1,0:T(8,128)(2,1)}, u32[]{:S(2)}) copy-start(bf16[320,2048]{1,0:T(8,128)(2,1)} %param.17) | copy-start | bytes 3932164
  7.2 2.4 copy-start.4
  9.7 9.8 %copy-start.10 = (s32[16]{0:T(128)S(1)}, s32[16]{0:T(128)}, u32[]{:S(2)}) copy-start(s32[16]{0:T(128)} %param.21) | copy-start | bytes 196
  9.7 9.8 %copy-start.13 = (s32[16]{0:T(128)S(1)}, s32[16]{0:T(128)}, u32[]{:S(2)}) copy-start(s32[16]{0:T(128)} %param.22) | copy-start | bytes 196
  10.7 11.0 %collective-permute-start = (bf16[1,5,256,128]{3,2,1,0:T(8,128)(2,1)}, bf16[1,5,256,128]{3,2,1,0:T(8,128)(2,1)}, u32[]{:S(2)}, u32[]{:S(2)}) collective-permute-start(bf16[1,5,256,128]{3,2,1,0:T(8,128)(2,1)} %get-tuple-element.44), channel_id=1, source_target_pairs={{0,4},{4,0},{8,12},{12,8},{16,20},{20,16},{24,28},{28,24},{1,5},{5... | collective-permute-start | bytes 983048 | tf_op jit(solution)/shard_map/ppermute | solution.py:19
  13.7 23.8 %collective-permute-start.1 = (bf16[1,5,256,128]{3,2,1,0:T(8,128)(2,1)S(1)}, bf16[1,5,256,128]{3,2,1,0:T(8,128)(2,1)}, u32[]{:S(2)}, u32[]{:S(2)}) collective-permute-start(bf16[1,5,256,128]{3,2,1,0:T(8,128)(2,1)S(1)} %get-tuple-element.43), channel_id=1, source_target_pairs={{0,8},{4,12},{8,0},{12,4},{16,24},{20,28},{24,16},{28,20},{1,9},{5... | collective-permute-start | bytes 983048 | tf_op jit(solution)/shard_map/ppermute | solution.py:19
  15.3 26.9 %collective-permute-start.2 = (bf16[1,5,256,128]{3,2,1,0:T(8,128)(2,1)S(1)}, bf16[1,5,256,128]{3,2,1,0:T(8,128)(2,1)}, u32[]{:S(2)}, u32[]{:S(2)}) collective-permute-start(bf16[1,5,256,128]{3,2,1,0:T(8,128)(2,1)S(1)} %get-tuple-element.42), channel_id=1, source_target_pairs={{0,12},{4,8},{8,4},{12,0},{16,28},{20,24},{24,20},{28,16},{1,13},{... | collective-permute-start | bytes 983048 | tf_op jit(solution)/shard_map/ppermute | solution.py:19
  15.3 28.6 %collective-permute-start.3 = (bf16[1,5,256,128]{3,2,1,0:T(8,128)(2,1)S(1)}, bf16[1,5,256,128]{3,2,1,0:T(8,128)(2,1)}, u32[]{:S(2)}, u32[]{:S(2)}) collective-permute-start(bf16[1,5,256,128]{3,2,1,0:T(8,128)(2,1)S(1)} %get-tuple-element.41), channel_id=1, source_target_pairs={{0,16},{4,20},{8,24},{12,28},{16,0},{20,4},{24,8},{28,12},{1,17},{... | collective-permute-start | bytes 983048 | tf_op jit(solution)/shard_map/ppermute | solution.py:19
  18.2 45.1 %collective-permute-start.4 = (bf16[1,5,256,128]{3,2,1,0:T(8,128)(2,1)S(1)}, bf16[1,5,256,128]{3,2,1,0:T(8,128)(2,1)}, u32[]{:S(2)}, u32[]{:S(2)}) collective-permute-start(bf16[1,5,256,128]{3,2,1,0:T(8,128)(2,1)S(1)} %get-tuple-element.40), channel_id=1, source_target_pairs={{0,20},{4,16},{8,28},{12,24},{16,4},{20,0},{24,12},{28,8},{1,21},{... | collective-permute-start | bytes 983048 | tf_op jit(solution)/shard_map/ppermute | solution.py:19
  21.7 43.4 %collective-permute-start.5 = (bf16[1,5,256,128]{3,2,1,0:T(8,128)(2,1)S(1)}, bf16[1,5,256,128]{3,2,1,0:T(8,128)(2,1)S(1)}, u32[]{:S(2)}, u32[]{:S(2)}) collective-permute-start(bf16[1,5,256,128]{3,2,1,0:T(8,128)(2,1)S(1)} %get-tuple-element.46), channel_id=1, source_target_pairs={{0,24},{4,28},{8,16},{12,20},{16,8},{20,12},{24,0},{28,4},{1,25},{... | collective-permute-start | bytes 983048 | tf_op jit(solution)/shard_map/ppermute | solution.py:19
  37.5 28.3 %collective-permute-start.6 = (bf16[1,5,256,128]{3,2,1,0:T(8,128)(2,1)S(1)}, bf16[1,5,256,128]{3,2,1,0:T(8,128)(2,1)S(1)}, u32[]{:S(2)}, u32[]{:S(2)}) collective-permute-start(bf16[1,5,256,128]{3,2,1,0:T(8,128)(2,1)S(1)} %get-tuple-element.39), channel_id=1, source_target_pairs={{0,28},{4,24},{8,20},{12,16},{16,12},{20,8},{24,4},{28,0},{1,29},{... | collective-permute-start | bytes 983048 | tf_op jit(solution)/shard_map/ppermute | solution.py:19
  77.3 128.7 %all-to-all-start = ((bf16[16,5,256,128]{3,2,1,0:T(8,128)(2,1)}), bf16[16,5,256,128]{3,2,1,0:T(8,128)(2,1)}, u32[]{:S(2)}, u32[]{:S(2)}) async-start(bf16[16,5,256,128]{3,2,1,0:T(8,128)(2,1)} %select_select_fusion), calls=%async_computation | async-start | bytes 10485760 | tf_op jit(solution)/shard_map/all_to_all | solution.py:95
  90.8 4.7 %copy-start.2 = (bf16[2,256,2048]{2,1,0:T(8,128)(2,1)S(1)}, bf16[2,256,2048]{2,1,0:T(8,128)(2,1)}, u32[]{:S(2)}) copy-start(bf16[2,256,2048]{2,1,0:T(8,128)(2,1)} %param.13) | copy-start | bytes 6291460
  90.8 260.1 %all-reduce.3.cloned.1.call-start = ((), (), s32[]{:S(2)}) async-start(), calls=%async_computation.1 | async-start | bytes 8388608 | tf_op jit(solution)/shard_map/psum | solution.py:144
  90.9 5.1 %copy-start.16 = (f32[2048]{0:T(1024)S(1)}, f32[2048]{0:T(1024)}, u32[]{:S(2)}) copy-start(f32[2048]{0:T(1024)} %param.14) | copy-start | bytes 24580
  96.0 5.2 %copy-start.14 = (s32[16]{0:T(128)S(1)}, s32[16]{0:T(128)}, u32[]{:S(2)}) copy-start(s32[16]{0:T(128)} %param.23) | copy-start | bytes 196
  99.4 1.1 copy-start.5
  102.5 2.8 copy-start.6
  102.5 2.8 copy-start.11
  102.5 2.8 copy-start.12
  104.9 1.0 copy-start.7
  210.1 4.2 %copy-start.1 = (bf16[2,5,2048,128]{3,2,1,0:T(8,128)(2,1)}, bf16[2,5,2048,128]{3,2,1,0:T(8,128)(2,1)S(1)}, u32[]{:S(2)}) copy-start(bf16[2,5,2048,128]{3,2,1,0:T(8,128)(2,1)S(1)} %bitcast_select_fusion) | copy-start | bytes 15728644
  257.8 6.4 %copy-start.8 = (bf16[5,64,256]{2,1,0:T(8,128)(2,1)S(1)}, bf16[5,64,256]{2,1,0:T(8,128)(2,1)}, u32[]{:S(2)}) copy-start(bf16[5,64,256]{2,1,0:T(8,128)(2,1)} %fusion.37) | copy-start | bytes 491524
  267.4 0.7 copy-start.15
  268.2 5.6 %copy-start.9 = (s32[4]{0:T(128)S(1)}, s32[4]{0:T(128)}, u32[]{:S(2)}) copy-start(s32[4]{0:T(128)} %constant.248) | copy-start | bytes 52
  299.1 51.8 %copy-start.3 = (bf16[2,256,2048]{2,1,0:T(8,128)(2,1)S(1)}, bf16[2,256,2048]{2,1,0:T(8,128)(2,1)}, u32[]{:S(2)}) copy-start(bf16[2,256,2048]{2,1,0:T(8,128)(2,1)} %param.13) | copy-start | bytes 6291460
  301.9 16.3 %collective-permute-start.7 = (bf16[2,5,288,128]{3,2,1,0:T(8,128)(2,1)}, bf16[2,5,288,128]{3,2,1,0:T(8,128)(2,1)}, u32[]{:S(2)}, u32[]{:S(2)}) collective-permute-start(bf16[2,5,288,128]{3,2,1,0:T(8,128)(2,1)} %get-tuple-element.36), channel_id=1, source_target_pairs={{0,4},{4,0},{8,12},{12,8},{16,20},{20,16},{24,28},{28,24},{1,5},{5... | collective-permute-start | bytes 2211848 | tf_op jit(solution)/shard_map/ppermute | solution.py:27
Sparse Core Ops, SparseCore 0:
  267.6 83.3 all-reduce.2
